TPU v7x, 512 devices: a whole 4x4x16 slice. The times are simulated.
512 devices in a mesh: row: 32 (over y, x, core), col: 16 (over z).
Axes of the slice: x: 4, y: 4, z: 16, core: 2. Of those that a mesh axis runs over, the one named last changes fastest.
Arguments:
- noise: bfloat16 [16384, 128], P('row'), may hold values from -6 to 6
- w_first: bfloat16 [128, 512], replicated, may hold values from -0.5 to 0.5
- w_second: bfloat16 [512, 1024], replicated, may hold values from -0.25 to 0.25
- history: bfloat16 [16384, 1024], P('col'), may hold values from -4 to 4
Outputs:
- grad_first: float32 [128, 512], replicated
- grad_second: float32 [512, 1024], P(None, 'col')
All inputs are finite; a program needn't handle non-finite values.
Results may differ from a plain program's by a relative error of at most 0.00085.
Values sent between devices are 32-bit elements; how exact they have to be, the bound alone decides.
A program may use at most 64 MiB of HBM per device.

v0:
```python
import math
import jax
import jax.numpy as jnp
from jax import lax
from jax.sharding import PartitionSpec as P

SWEEPS = 3
EPSILON = 0.01


def row_lse(scores):
    maxima = lax.pmax(jnp.max(scores, axis=1), "col")
    totals = lax.psum(jnp.sum(jnp.exp(scores - maxima[:, None]), axis=1), "col")
    return maxima + jnp.log(totals)


def col_lse(scores):
    maxima = lax.pmax(jnp.max(scores, axis=0), "row")
    totals = lax.psum(jnp.sum(jnp.exp(scores - maxima[None, :]), axis=0), "row")
    return maxima + jnp.log(totals)


def shards(noise, w_first, w_second, history):
    gen_total = noise.shape[0] * lax.axis_size("row")
    hist_total = history.shape[0] * lax.axis_size("col")
    width = w_second.shape[1]
    slice_width = width // lax.axis_size("col")
    col_start = lax.axis_index("col") * slice_width
    preact = jnp.dot(noise, w_first, preferred_element_type=jnp.float32)
    hidden = jax.nn.silu(preact).astype(jnp.bfloat16)
    surface = jnp.dot(hidden, w_second, preferred_element_type=jnp.float32).astype(jnp.bfloat16)
    surf_f = surface.astype(jnp.float32)
    hist_f = history.astype(jnp.float32)
    surf_sq = jnp.sum(surf_f * surf_f, axis=1)
    hist_sq = jnp.sum(hist_f * hist_f, axis=1)
    inner = lax.dot_general(
        surface, history, (((1,), (1,)), ((), ())), preferred_element_type=jnp.float32
    )
    cost_tile = (surf_sq[:, None] + hist_sq[None, :] - 2.0 * inner) / width
    f_pot = jnp.zeros((noise.shape[0],), jnp.float32)
    g_pot = jnp.zeros((history.shape[0],), jnp.float32)
    for sweep_no in range(SWEEPS):
        g_pot = -EPSILON * (-math.log(gen_total) + col_lse((f_pot[:, None] - cost_tile) / EPSILON))
        f_pot = -EPSILON * (-math.log(hist_total) + row_lse((g_pot[None, :] - cost_tile) / EPSILON))
    weights = (
        jnp.exp((f_pot[:, None] + g_pot[None, :] - cost_tile) / EPSILON) / hist_total
    ).astype(jnp.bfloat16)
    partial_value = jnp.dot(weights, history, preferred_element_type=jnp.float32)
    scale = 1.0 / math.sqrt(gen_total)
    barycentre = lax.psum(partial_value, "col")
    d_surface = ((surf_f - barycentre) * scale).astype(jnp.bfloat16)
    d_hidden = lax.dot_general(
        d_surface, w_second, (((1,), (1,)), ((), ())), preferred_element_type=jnp.float32
    )
    d_slice = lax.dynamic_slice_in_dim(d_surface, col_start, slice_width, 1)
    sigma = jax.nn.sigmoid(preact)
    d_preact = (d_hidden * sigma * (1.0 + preact * (1.0 - sigma))).astype(jnp.bfloat16)
    first_term = lax.dot_general(
        noise, d_preact, (((0,), (0,)), ((), ())), preferred_element_type=jnp.float32
    )
    second_term = lax.dot_general(
        hidden, d_slice, (((0,), (0,)), ((), ())), preferred_element_type=jnp.float32
    )
    grad_first, grad_second = lax.psum((first_term, second_term), "row")
    return (grad_first, grad_second)


def solution(mesh):
    placed = (P("row", None), P(), P(), P("col", None))
    return jax.shard_map(
        shards, mesh=mesh, in_specs=placed, out_specs=(P(), P(None, "col")), check_vma=False
    )
```

profile of v0, /device:TPU:1, one launch (start us, length us, event | category | flops | bytes accessed | tf_op | source)
XLA Modules:
  0.0 862.4 jit_solution(6891692069466334634)
XLA Ops:
  7.2 0.0 copy-start
  7.2 0.0 copy-start.7
  7.2 0.0 copy-start.6
  7.2 0.0 all-reduce.4.cloned.1.call-start
  7.2 2.2 multiply_reduce_fusion
  9.4 0.0 copy-done.7
  9.4 0.0 copy-done.6
  9.4 1.3 multiply_convert_fusion.2
  10.8 0.0 copy-start.4
  10.8 0.0 copy-start.1
  10.8 0.0 copy-done
  10.8 0.8 fusion
  11.6 0.0 copy-start.2
  11.6 0.0 copy-done.4
  11.6 1.0 copy-done.1
  12.5 1.5 fusion.3
  14.1 0.0 copy-done.2
  14.1 68.9 %pmax.42 = f32[1024]{0:T(1024)S(1)} all-reduce(f32[1024]{0:T(1024)S(1)} %get-tuple-element.10), channel_id=1, replica_groups=mesh['row'=32,'col'=16] {'row'}, use_global_device_ids=true, to_apply=%region_3.4 | all-reduce | flops 1024 | bytes 8192 | tf_op jit(solution)/shard_map/pmax | solution.py:18
  83.0 0.4 exponential_reduce_fusion.5
  83.4 62.7 %psum.63 = f32[1024]{0:T(1024)S(1)} all-reduce(f32[1024]{0:T(1024)S(1)} %exponential_reduce_fusion.5), channel_id=1, replica_groups=mesh['row'=32,'col'=16] {'row'}, use_global_device_ids=true, to_apply=%region_5.6 | all-reduce | flops 1024 | bytes 8192 | tf_op jit(solution)/shard_map/psum | solution.py:19
  146.1 0.3 fusion.4
  146.4 28.8 %pmax.43 = f32[512]{0:T(512)S(1)} all-reduce(f32[512]{0:T(512)S(1)} %fusion.4), channel_id=1, replica_groups=mesh['row'=32,'col'=16] {'col'}, use_global_device_ids=true, to_apply=%region_7.8 | all-reduce | flops 512 | bytes 4096 | tf_op jit(solution)/shard_map/pmax | solution.py:12
  175.2 0.6 exponential_reduce_fusion.4
  175.7 20.1 %psum.64 = f32[512]{0:T(512)S(1)} all-reduce(f32[512]{0:T(512)S(1)} %exponential_reduce_fusion.4), channel_id=1, replica_groups=mesh['row'=32,'col'=16] {'col'}, use_global_device_ids=true, to_apply=%region_9.10 | all-reduce | flops 512 | bytes 4096 | tf_op jit(solution)/shard_map/psum | solution.py:13
  195.8 0.3 fusion.5
  196.1 76.7 %pmax.44 = f32[1024]{0:T(1024)S(1)} all-reduce(f32[1024]{0:T(1024)S(1)} %fusion.5), channel_id=1, replica_groups=mesh['row'=32,'col'=16] {'row'}, use_global_device_ids=true, to_apply=%region_11.12 | all-reduce | flops 1024 | bytes 8192 | tf_op jit(solution)/shard_map/pmax | solution.py:18
  272.8 0.5 exponential_reduce_fusion.3
  273.3 62.7 %psum.65 = f32[1024]{0:T(1024)S(1)} all-reduce(f32[1024]{0:T(1024)S(1)} %exponential_reduce_fusion.3), channel_id=1, replica_groups=mesh['row'=32,'col'=16] {'row'}, use_global_device_ids=true, to_apply=%region_13.14 | all-reduce | flops 1024 | bytes 8192 | tf_op jit(solution)/shard_map/psum | solution.py:19
  335.9 0.3 fusion.6
  336.2 22.0 %pmax.45 = f32[512]{0:T(512)S(1)} all-reduce(f32[512]{0:T(512)S(1)} %fusion.6), channel_id=1, replica_groups=mesh['row'=32,'col'=16] {'col'}, use_global_device_ids=true, to_apply=%region_15.16 | all-reduce | flops 512 | bytes 4096 | tf_op jit(solution)/shard_map/pmax | solution.py:12
  358.2 0.6 exponential_reduce_fusion.2
  358.8 20.1 %psum.66 = f32[512]{0:T(512)S(1)} all-reduce(f32[512]{0:T(512)S(1)} %exponential_reduce_fusion.2), channel_id=1, replica_groups=mesh['row'=32,'col'=16] {'col'}, use_global_device_ids=true, to_apply=%region_17.18 | all-reduce | flops 512 | bytes 4096 | tf_op jit(solution)/shard_map/psum | solution.py:13
  378.9 0.3 fusion.7
  379.2 76.7 %pmax.46 = f32[1024]{0:T(1024)S(1)} all-reduce(f32[1024]{0:T(1024)S(1)} %fusion.7), channel_id=1, replica_groups=mesh['row'=32,'col'=16] {'row'}, use_global_device_ids=true, to_apply=%region_19.20 | all-reduce | flops 1024 | bytes 8192 | tf_op jit(solution)/shard_map/pmax | solution.py:18
  455.8 0.5 exponential_reduce_fusion.1
  456.3 62.7 %psum.67 = f32[1024]{0:T(1024)S(1)} all-reduce(f32[1024]{0:T(1024)S(1)} %exponential_reduce_fusion.1), channel_id=1, replica_groups=mesh['row'=32,'col'=16] {'row'}, use_global_device_ids=true, to_apply=%region_21.22 | all-reduce | flops 1024 | bytes 8192 | tf_op jit(solution)/shard_map/psum | solution.py:19
  519.0 0.3 fusion.8
  519.3 22.0 %pmax.47 = f32[512]{0:T(512)S(1)} all-reduce(f32[512]{0:T(512)S(1)} %fusion.8), channel_id=1, replica_groups=mesh['row'=32,'col'=16] {'col'}, use_global_device_ids=true, to_apply=%region_23.24 | all-reduce | flops 512 | bytes 4096 | tf_op jit(solution)/shard_map/pmax | solution.py:12
  541.3 0.6 exponential_reduce_fusion
  541.9 20.1 %psum.68 = f32[512]{0:T(512)S(1)} all-reduce(f32[512]{0:T(512)S(1)} %exponential_reduce_fusion), channel_id=1, replica_groups=mesh['row'=32,'col'=16] {'col'}, use_global_device_ids=true, to_apply=%region_25.26 | all-reduce | flops 512 | bytes 4096 | tf_op jit(solution)/shard_map/psum | solution.py:13
  562.0 4.2 fusion.13
  566.2 0.0 copy-start.3
  566.2 0.0 all-reduce.4.cloned.1.call-update
  566.2 0.0 all-reduce.6.cloned.1.call-start
  566.2 141.2 %all-reduce.4.cloned.1.call-done = f32[512,1024]{1,0:T(8,128)} async-done(((f32[512,1024]{1,0:T(8,128)}), f32[512,1024]{1,0:T(8,128)}) %all-reduce.4.cloned.1.call-update) | async-done | bytes 2097168 | tf_op jit(solution)/shard_map/psum | solution.py:50
  707.5 0.0 copy-done.3
  707.5 0.0 copy-start.5
  707.5 2.0 fusion.2
  709.5 0.0 copy-done.5
  709.5 1.0 fusion.22
  710.5 3.1 fusion.12
  713.6 0.0 all-reduce.6.cloned.1.call-update
  713.6 138.6 %all-reduce.6.cloned.1.call-done = (f32[128,512]{0,1:T(8,128)}, f32[512,64]{0,1:T(8,128)}) async-done(((f32[128,512]{0,1:T(8,128)}, f32[512,64]{0,1:T(8,128)}), (f32[128,512]{0,1:T(8,128)}, f32[512,64]{0,1:T(8,128)})) %all-reduce.6.cloned.1.call-update) | async-done | bytes 393232 | tf_op jit(solution)/shard_map/psum | solution.py:64
  852.2 1.8 copy.6
  854.0 1.6 copy.10
  (6 shorter events, 0.1 us)
Async XLA Ops:
  7.2 3.6 copy-start
  7.2 2.2 copy-start.7
  7.2 2.2 copy-start.6
  7.2 700.3 %all-reduce.4.cloned.1.call-start = ((), (), s32[]{:S(2)}) async-start(), calls=%async_computation | async-start | bytes 4194304 | tf_op jit(solution)/shard_map/psum | solution.py:50
  10.8 0.8 copy-start.4
  10.8 1.8 copy-start.1
  11.6 2.5 copy-start.2
  566.2 141.3 %copy-start.3 = (bf16[512,1024]{1,0:T(8,128)(2,1)S(1)}, bf16[512,1024]{1,0:T(8,128)(2,1)}, u32[]{:S(2)}) copy-start(bf16[512,1024]{1,0:T(8,128)(2,1)} %copy-done.2) | copy-start | bytes 3145732
  566.2 286.0 %all-reduce.6.cloned.1.call-start = ((), (), s32[]{:S(2)}) async-start(), calls=%async_computation.1 | async-start | bytes 786432 | tf_op jit(solution)/shard_map/psum | solution.py:64
  707.5 2.0 copy-start.5
Sparse Core Ops, SparseCore 0:
  566.3 141.1 all-reduce.3
  713.7 138.3 all-reduce.5
where the time goes:
time: 863 us; the launch traced here: 862 us
  blocking collectives  543 us (63%)
  waiting for transfers between devices  280 us (32%)
  between operations  14.2 us (2%)
  matrix products  12 us (1%)
  other arithmetic  8.78 us (1%)
    pmax x3, blocking collectives, col_lse(): maxima = lax.pmax(jnp.max(scores, axis=0), 'row')  222 us
    psum x3, blocking collectives, col_lse(): totals = lax.psum(jnp.sum(jnp.exp(scores - maxima[None, :]), axis=0), 'row')  188 us
    psum x1, waiting for transfers between devices, shards(): barycentre = lax.psum(partial_value, 'col')  141 us
    psum x1, waiting for transfers between devices, shards(): grad_first, grad_second = lax.psum((first_term, second_term), 'row')  139 us
    pmax x3, blocking collectives, row_lse(): maxima = lax.pmax(jnp.max(scores, axis=1), 'col')  72.8 us
    psum x3, blocking collectives, row_lse(): totals = lax.psum(jnp.sum(jnp.exp(scores - maxima[:, None]), axis=1), 'col')  60.2 us
  transfers between devices with their start and end apart: 2, of which 2 were waited for; matrix products, arithmetic and copies ran while one was open for 0% of the time, Pallas kernels for 0%

commit v1 on v0

--- a/solution.py
+++ b/solution.py
@@ -47,7 +47,11 @@
     ).astype(jnp.bfloat16)
     partial_value = jnp.dot(weights, history, preferred_element_type=jnp.float32)
     scale = 1.0 / math.sqrt(gen_total)
-    barycentre = lax.psum(partial_value, "col")
+    barycentre = partial_value
+    for hop in (1, 2, 4, 8):
+        barycentre = barycentre + lax.ppermute(
+            barycentre, "col", [(dev, dev ^ hop) for dev in range(16)]
+        )
     d_surface = ((surf_f - barycentre) * scale).astype(jnp.bfloat16)
     d_hidden = lax.dot_general(
         d_surface, w_second, (((1,), (1,)), ((), ())), preferred_element_type=jnp.float32

time: 863 us -> 1200 us (1.39)
  waiting for transfers between devices: 280 us -> 601 us
  starting transfers between devices: 0.08 us -> 16.3 us
    ppermute x0 -> x4, waiting for transfers between devices: none -> 450 us  [shards(): lax.ppermute(barycentre, 'col', [(dev, dev ^ hop) for dev in range(16)])]
    psum x1 -> x0, waiting for transfers between devices: 141 us -> none  [shards(): barycentre = lax.psum(partial_value, 'col')]
    ppermute x0 -> x4, starting transfers between devices: none -> 16.3 us  [shards(): lax.ppermute(barycentre, 'col', [(dev, dev ^ hop) for dev in range(16)])]
    psum x1, waiting for transfers between devices: 139 us -> 152 us  [shards(): grad_first, grad_second = lax.psum((first_term, second_term), 'row')]
  transfers between devices with their start and end apart: 2 -> 5, of which waited for: 2 -> 5; matrix products, arithmetic and copies ran while one was open for 0% -> 0% of each run, Pallas kernels for 0% -> 0%
where the time goes in v1:
time: 1200 us
  waiting for transfers between devices  601 us (50%)
  blocking collectives  543 us (45%)
  starting transfers between devices  16.3 us (1%)
  between operations  14.2 us (1%)
    ppermute x4, waiting for transfers between devices, shards(): lax.ppermute(barycentre, 'col', [(dev, dev ^ hop) for dev in range(16)])  450 us
    pmax x3, blocking collectives, col_lse(): maxima = lax.pmax(jnp.max(scores, axis=0), 'row')  222 us
    psum x3, blocking collectives, col_lse(): totals = lax.psum(jnp.sum(jnp.exp(scores - maxima[None, :]), axis=0), 'row')  188 us
    psum x1, waiting for transfers between devices, shards(): grad_first, grad_second = lax.psum((first_term, second_term), 'row')  152 us
    pmax x3, blocking collectives, row_lse(): maxima = lax.pmax(jnp.max(scores, axis=1), 'col')  72.8 us
    psum x3, blocking collectives, row_lse(): totals = lax.psum(jnp.sum(jnp.exp(scores - maxima[:, None]), axis=1), 'col')  60.2 us
  transfers between devices with their start and end apart: 5, of which 5 were waited for; matrix products, arithmetic and copies ran while one was open for 0% of the time, Pallas kernels for 0%

profile of v1, /device:TPU:1, one launch (start us, length us, event | category | flops | bytes accessed | tf_op | source)
XLA Modules:
  0.0 1202.3 jit_solution(4471996700964385678)
XLA Ops:
  7.2 0.0 copy-start
  7.2 0.0 copy-start.7
  7.2 0.0 copy-start.6
  7.2 0.0 all-reduce.3.cloned.1.call-start
  7.2 2.2 multiply_reduce_fusion
  9.4 0.0 copy-done.7
  9.4 0.0 copy-done.6
  9.4 1.3 multiply_convert_fusion.2
  10.8 0.0 copy-start.4
  10.8 0.0 copy-start.1
  10.8 0.0 copy-done
  10.8 0.8 fusion
  11.6 0.0 copy-start.3
  11.6 0.0 copy-done.4
  11.6 1.0 copy-done.1
  12.5 1.5 fusion.3
  14.1 0.0 copy-done.3
  14.1 68.9 %pmax.42 = f32[1024]{0:T(1024)S(1)} all-reduce(f32[1024]{0:T(1024)S(1)} %get-tuple-element.10), channel_id=1, replica_groups=mesh['row'=32,'col'=16] {'row'}, use_global_device_ids=true, to_apply=%region_3.4 | all-reduce | flops 1024 | bytes 8192 | tf_op jit(solution)/shard_map/pmax | solution.py:18
  83.0 0.4 exponential_reduce_fusion.5
  83.4 62.7 %psum.56 = f32[1024]{0:T(1024)S(1)} all-reduce(f32[1024]{0:T(1024)S(1)} %exponential_reduce_fusion.5), channel_id=1, replica_groups=mesh['row'=32,'col'=16] {'row'}, use_global_device_ids=true, to_apply=%region_5.6 | all-reduce | flops 1024 | bytes 8192 | tf_op jit(solution)/shard_map/psum | solution.py:19
  146.1 0.3 fusion.4
  146.4 28.8 %pmax.43 = f32[512]{0:T(512)S(1)} all-reduce(f32[512]{0:T(512)S(1)} %fusion.4), channel_id=1, replica_groups=mesh['row'=32,'col'=16] {'col'}, use_global_device_ids=true, to_apply=%region_7.8 | all-reduce | flops 512 | bytes 4096 | tf_op jit(solution)/shard_map/pmax | solution.py:12
  175.2 0.6 exponential_reduce_fusion.4
  175.7 20.1 %psum.57 = f32[512]{0:T(512)S(1)} all-reduce(f32[512]{0:T(512)S(1)} %exponential_reduce_fusion.4), channel_id=1, replica_groups=mesh['row'=32,'col'=16] {'col'}, use_global_device_ids=true, to_apply=%region_9.10 | all-reduce | flops 512 | bytes 4096 | tf_op jit(solution)/shard_map/psum | solution.py:13
  195.8 0.3 fusion.5
  196.1 76.7 %pmax.44 = f32[1024]{0:T(1024)S(1)} all-reduce(f32[1024]{0:T(1024)S(1)} %fusion.5), channel_id=1, replica_groups=mesh['row'=32,'col'=16] {'row'}, use_global_device_ids=true, to_apply=%region_11.12 | all-reduce | flops 1024 | bytes 8192 | tf_op jit(solution)/shard_map/pmax | solution.py:18
  272.8 0.5 exponential_reduce_fusion.3
  273.3 62.7 %psum.58 = f32[1024]{0:T(1024)S(1)} all-reduce(f32[1024]{0:T(1024)S(1)} %exponential_reduce_fusion.3), channel_id=1, replica_groups=mesh['row'=32,'col'=16] {'row'}, use_global_device_ids=true, to_apply=%region_13.14 | all-reduce | flops 1024 | bytes 8192 | tf_op jit(solution)/shard_map/psum | solution.py:19
  336.0 0.3 fusion.6
  336.2 22.0 %pmax.45 = f32[512]{0:T(512)S(1)} all-reduce(f32[512]{0:T(512)S(1)} %fusion.6), channel_id=1, replica_groups=mesh['row'=32,'col'=16] {'col'}, use_global_device_ids=true, to_apply=%region_15.16 | all-reduce | flops 512 | bytes 4096 | tf_op jit(solution)/shard_map/pmax | solution.py:12
  358.3 0.6 exponential_reduce_fusion.2
  358.8 20.1 %psum.59 = f32[512]{0:T(512)S(1)} all-reduce(f32[512]{0:T(512)S(1)} %exponential_reduce_fusion.2), channel_id=1, replica_groups=mesh['row'=32,'col'=16] {'col'}, use_global_device_ids=true, to_apply=%region_17.18 | all-reduce | flops 512 | bytes 4096 | tf_op jit(solution)/shard_map/psum | solution.py:13
  378.9 0.3 fusion.7
  379.2 76.7 %pmax.46 = f32[1024]{0:T(1024)S(1)} all-reduce(f32[1024]{0:T(1024)S(1)} %fusion.7), channel_id=1, replica_groups=mesh['row'=32,'col'=16] {'row'}, use_global_device_ids=true, to_apply=%region_19.20 | all-reduce | flops 1024 | bytes 8192 | tf_op jit(solution)/shard_map/pmax | solution.py:18
  455.8 0.5 exponential_reduce_fusion.1
  456.3 62.7 %psum.60 = f32[1024]{0:T(1024)S(1)} all-reduce(f32[1024]{0:T(1024)S(1)} %exponential_reduce_fusion.1), channel_id=1, replica_groups=mesh['row'=32,'col'=16] {'row'}, use_global_device_ids=true, to_apply=%region_21.22 | all-reduce | flops 1024 | bytes 8192 | tf_op jit(solution)/shard_map/psum | solution.py:19
  519.0 0.3 fusion.8
  519.3 22.0 %pmax.47 = f32[512]{0:T(512)S(1)} all-reduce(f32[512]{0:T(512)S(1)} %fusion.8), channel_id=1, replica_groups=mesh['row'=32,'col'=16] {'col'}, use_global_device_ids=true, to_apply=%region_23.24 | all-reduce | flops 512 | bytes 4096 | tf_op jit(solution)/shard_map/pmax | solution.py:12
  541.3 0.6 exponential_reduce_fusion
  541.9 20.1 %psum.61 = f32[512]{0:T(512)S(1)} all-reduce(f32[512]{0:T(512)S(1)} %exponential_reduce_fusion), channel_id=1, replica_groups=mesh['row'=32,'col'=16] {'col'}, use_global_device_ids=true, to_apply=%region_25.26 | all-reduce | flops 512 | bytes 4096 | tf_op jit(solution)/shard_map/psum | solution.py:13
  562.0 2.9 fusion.13
  564.9 3.4 collective-permute-start
  568.2 31.0 %collective-permute-done = f32[512,1024]{1,0:T(8,128)S(1)} collective-permute-done((f32[512,1024]{1,0:T(8,128)S(1)}, f32[512,1024]{1,0:T(8,128)S(1)}, u32[]{:S(2)}, u32[]{:S(2)}) %collective-permute-start) | collective-permute-done | bytes 2097184 | tf_op jit(solution)/shard_map/ppermute | solution.py:52
  599.3 0.6 add.117
  599.8 1.9 collective-permute-start.1
  601.7 84.5 %collective-permute-done.1 = f32[512,1024]{1,0:T(8,128)S(1)} collective-permute-done((f32[512,1024]{1,0:T(8,128)S(1)}, f32[512,1024]{1,0:T(8,128)S(1)}, u32[]{:S(2)}, u32[]{:S(2)}) %collective-permute-start.1) | collective-permute-done | bytes 2097184 | tf_op jit(solution)/shard_map/ppermute | solution.py:52
  686.2 0.6 add.118
  686.8 3.0 collective-permute-start.2
  689.8 225.3 %collective-permute-done.2 = f32[512,1024]{1,0:T(8,128)S(1)} collective-permute-done((f32[512,1024]{1,0:T(8,128)S(1)}, f32[512,1024]{1,0:T(8,128)S(1)}, u32[]{:S(2)}, u32[]{:S(2)}) %collective-permute-start.2) | collective-permute-done | bytes 2097184 | tf_op jit(solution)/shard_map/ppermute | solution.py:52
  915.1 0.4 add.119
  915.5 8.0 collective-permute-start.3
  923.5 0.0 copy-start.5
  923.6 109.0 %collective-permute-done.3 = f32[512,1024]{1,0:T(8,128)} collective-permute-done((f32[512,1024]{1,0:T(8,128)S(1)}, f32[512,1024]{1,0:T(8,128)}, u32[]{:S(2)}, u32[]{:S(2)}) %collective-permute-start.3) | collective-permute-done | bytes 2097184 | tf_op jit(solution)/shard_map/ppermute | solution.py:52
  1032.6 2.5 fusion.2
  1035.1 0.0 copy-start.2
  1035.1 1.0 copy-done.2
  1036.1 0.0 copy-done.5
  1036.1 1.0 fusion.22
  1037.0 3.4 fusion.12
  1040.5 0.0 all-reduce.3.cloned.1.call-update
  1040.5 151.6 %all-reduce.3.cloned.1.call-done = (f32[128,512]{0,1:T(8,128)}, f32[512,64]{0,1:T(8,128)}) async-done(((f32[128,512]{0,1:T(8,128)}, f32[512,64]{0,1:T(8,128)}), (f32[128,512]{0,1:T(8,128)}, f32[512,64]{0,1:T(8,128)})) %all-reduce.3.cloned.1.call-update) | async-done | bytes 393232 | tf_op jit(solution)/shard_map/psum | solution.py:68
  1192.1 1.8 copy.6
  1193.9 1.6 copy.9
  (6 shorter events, 0.1 us)
Async XLA Ops:
  7.2 3.6 copy-start
  7.2 2.2 copy-start.7
  7.2 2.2 copy-start.6
  7.2 1184.9 %all-reduce.3.cloned.1.call-start = ((), (), s32[]{:S(2)}) async-start(), calls=%async_computation | async-start | bytes 786432 | tf_op jit(solution)/shard_map/psum | solution.py:68
  10.8 0.8 copy-start.4
  10.8 1.8 copy-start.1
  11.6 2.5 copy-start.3
  564.9 34.4 %collective-permute-start = (f32[512,1024]{1,0:T(8,128)S(1)}, f32[512,1024]{1,0:T(8,128)S(1)}, u32[]{:S(2)}, u32[]{:S(2)}) collective-permute-start(f32[512,1024]{1,0:T(8,128)S(1)} %fusion.13), channel_id=1, source_target_pairs={{0,1},{1,0},{2,3},{3,2},{4,5},{5,4},{6,7},{7,6},{8,9},{9,8},{10,11... | collective-permute-start | bytes 6291464 | tf_op jit(solution)/shard_map/ppermute | solution.py:52
  599.8 86.4 %collective-permute-start.1 = (f32[512,1024]{1,0:T(8,128)S(1)}, f32[512,1024]{1,0:T(8,128)S(1)}, u32[]{:S(2)}, u32[]{:S(2)}) collective-permute-start(f32[512,1024]{1,0:T(8,128)S(1)} %add.117), channel_id=1, source_target_pairs={{0,2},{1,3},{2,0},{3,1},{4,6},{5,7},{6,4},{7,5},{8,10},{9,11},{10,... | collective-permute-start | bytes 6291464 | tf_op jit(solution)/shard_map/ppermute | solution.py:52
  686.8 228.3 %collective-permute-start.2 = (f32[512,1024]{1,0:T(8,128)S(1)}, f32[512,1024]{1,0:T(8,128)S(1)}, u32[]{:S(2)}, u32[]{:S(2)}) collective-permute-start(f32[512,1024]{1,0:T(8,128)S(1)} %add.118), channel_id=1, source_target_pairs={{0,4},{1,5},{2,6},{3,7},{4,0},{5,1},{6,2},{7,3},{8,12},{9,13},{10,... | collective-permute-start | bytes 6291464 | tf_op jit(solution)/shard_map/ppermute | solution.py:52
  915.5 117.0 %collective-permute-start.3 = (f32[512,1024]{1,0:T(8,128)S(1)}, f32[512,1024]{1,0:T(8,128)}, u32[]{:S(2)}, u32[]{:S(2)}) collective-permute-start(f32[512,1024]{1,0:T(8,128)S(1)} %add.119), channel_id=1, source_target_pairs={{0,8},{1,9},{2,10},{3,11},{4,12},{5,13},{6,14},{7,15},{8,0},{9,1},... | collective-permute-start | bytes 6291464 | tf_op jit(solution)/shard_map/ppermute | solution.py:52
  923.5 112.5 %copy-start.5 = (bf16[512,512]{1,0:T(8,128)(2,1)S(1)}, bf16[512,512]{1,0:T(8,128)(2,1)}, u32[]{:S(2)}) copy-start(bf16[512,512]{1,0:T(8,128)(2,1)} %copy-done.4) | copy-start | bytes 1572868
  1035.1 1.0 copy-start.2
Sparse Core Ops, SparseCore 0:
  1040.6 151.4 all-reduce.2
